TPU v7x, 32 devices: a whole 2x2x4 slice. The times are simulated.
32 devices in a mesh: row: 8 (over z, x), col: 4 (over y, core).
Axes of the slice: x: 2, y: 2, z: 4, core: 2. Of those that a mesh axis runs over, the one named last changes fastest.
Arguments:
- tokens: bfloat16 [64, 512, 512], P('row', 'col'), may hold values from -6 to 6
- ln1_gain: float32 [512], replicated, may hold values from 0.1 to 1.9
- w_qkv: bfloat16 [512, 1536], replicated
- rel_bias: float32 [16, 49], replicated, may hold values from -4 to 4
- w_proj: bfloat16 [512, 512], replicated, may hold values from -0.25 to 0.25
- ln2_gain: float32 [512], replicated, may hold values from 0.1 to 1.9
- w_up: bfloat16 [512, 2048], replicated, may hold values from -0.25 to 0.25
- w_down: bfloat16 [2048, 512], replicated, may hold values from -0.125 to 0.125
- merge_gain: float32 [2048], replicated, may hold values from 0.3 to 3
- w_merge: bfloat16 [2048, 1024], replicated, may hold values from -0.125 to 0.125
- cotangent: bfloat16 [32, 256, 1024], P('row', 'col'), may hold values from -6 to 6
Outputs:
- merged: bfloat16 [32, 256, 1024], P('row', 'col')
- grad_merge: float32 [2048, 1024], P(('row', 'col'))
- grad_down: float32 [2048, 512], P(('row', 'col'))
All inputs are finite; a program needn't handle non-finite values.
Results may differ from a plain program's by a relative error of at most 0.012.
Values may be sent and summed in bfloat16 or wider, within the bound.
A program may use at most 128 MiB of HBM per device.

v0:
```python
import jax
import jax.numpy as jnp
from jax import lax
from jax.sharding import PartitionSpec as P


def with_halo(cells, sides, width):
    for axis, dim in sides:
        count = lax.axis_size(axis)
        ends = count - 1
        head = lax.slice_in_dim(cells, 0, width, axis=dim)
        tail = lax.slice_in_dim(cells, cells.shape[dim] - width, cells.shape[dim], axis=dim)
        cells = jnp.concatenate(
            [
                lax.ppermute(tail, axis, [(i, (i + 1) % count) for i in range(ends)]),
                cells,
                lax.ppermute(head, axis, [((i + 1) % count, i) for i in range(ends)]),
            ],
            axis=dim,
        )
    return cells


def layer_norm(value, gain):
    mean = jnp.mean(value, axis=-1, keepdims=True)
    var = jnp.mean((value - mean) ** 2, axis=-1, keepdims=True)
    return (value - mean) / jnp.sqrt(var + 1e-05) * gain


def local(
    tokens,
    ln1_gain,
    w_qkv,
    rel_bias,
    w_proj,
    ln2_gain,
    w_up,
    w_down,
    merge_gain,
    w_merge,
    cotangent,
):
    rows, cols, width = tokens.shape
    heads = rel_bias.shape[0]
    head_dim = width // heads
    x_flat = tokens.astype(jnp.float32).reshape(-1, width)
    normed = layer_norm(x_flat, ln1_gain).astype(jnp.bfloat16)
    query = jnp.dot(normed, w_qkv[:, :width], preferred_element_type=jnp.float32).astype(
        jnp.bfloat16
    )
    query_t = query.reshape(rows, cols, heads, head_dim).transpose(0, 2, 3, 1)
    keyval = jnp.dot(normed, w_qkv[:, width:], preferred_element_type=jnp.float32).astype(
        jnp.bfloat16
    )
    keyval = keyval.reshape(rows, cols, 2 * width).transpose(0, 2, 1)
    padded = with_halo(keyval, (("row", 0), ("col", 2)), 3)
    padded = padded.reshape(rows + 6, 2, heads, head_dim, cols + 6)
    total_rows = rows * lax.axis_size("row")
    total_cols = cols * lax.axis_size("col")
    row_pos = lax.axis_index("row") * rows + jnp.arange(rows)
    col_pos = lax.axis_index("col") * cols + jnp.arange(cols)
    scores = []
    masks = []
    for di in range(7):
        for dj in range(7):
            key = padded[di : di + rows, 0, :, :, dj : dj + cols]
            scores.append(
                jnp.einsum("rhdc,rhdc->rhc", query_t, key, preferred_element_type=jnp.float32)
            )
            rows_ok = (row_pos + di - 3 >= 0) & (row_pos + di - 3 < total_rows)
            cols_ok = (col_pos + dj - 3 >= 0) & (col_pos + dj - 3 < total_cols)
            masks.append(rows_ok[:, None] & cols_ok[None, :])
    scale = 1.0 / jnp.sqrt(jnp.float32(head_dim))
    score = jnp.stack(scores, 0) * scale + rel_bias.T[:, None, :, None]
    valid = jnp.stack(masks, 0)[:, :, None, :]
    score = jnp.where(valid, score, -1e30)
    top = jnp.max(score, axis=0, keepdims=True)
    expo = jnp.where(valid, jnp.exp(score - top), 0.0)
    probs = (expo / jnp.sum(expo, axis=0, keepdims=True)).astype(jnp.bfloat16)
    attn = jnp.zeros((rows, heads, head_dim, cols), jnp.float32)
    offset = 0
    for di in range(7):
        for dj in range(7):
            value = padded[di : di + rows, 1, :, :, dj : dj + cols]
            attn = attn + jnp.einsum(
                "rhc,rhdc->rhdc", probs[offset], value, preferred_element_type=jnp.float32
            )
            offset += 1
    attn = attn.astype(jnp.bfloat16).transpose(0, 3, 1, 2).reshape(-1, width)
    h_one = (x_flat + jnp.dot(attn, w_proj, preferred_element_type=jnp.float32)).astype(
        jnp.bfloat16
    )
    normed2 = layer_norm(h_one.astype(jnp.float32), ln2_gain).astype(jnp.bfloat16)
    hidden = jax.nn.gelu(
        jnp.dot(normed2, w_up, preferred_element_type=jnp.float32), approximate=False
    ).astype(jnp.bfloat16)
    out_y = (
        h_one.astype(jnp.float32) + jnp.dot(hidden, w_down, preferred_element_type=jnp.float32)
    ).astype(jnp.bfloat16)
    joined = (
        out_y.reshape(rows // 2, 2, cols // 2, 2, width)
        .transpose(0, 2, 3, 1, 4)
        .reshape(-1, 4 * width)
        .astype(jnp.float32)
    )
    mean = jnp.mean(joined, axis=-1, keepdims=True)
    inv = 1.0 / jnp.sqrt(jnp.mean((joined - mean) ** 2, axis=-1, keepdims=True) + 1e-05)
    unit = (joined - mean) * inv
    merge_in = (unit * merge_gain).astype(jnp.bfloat16)
    merged = jnp.dot(merge_in, w_merge, preferred_element_type=jnp.float32).astype(jnp.bfloat16)
    merged = merged.reshape(rows // 2, cols // 2, 2 * width)
    cot = cotangent.reshape(-1, 2 * width)
    grad_m = jnp.dot(merge_in.T, cot, preferred_element_type=jnp.float32)
    grad_n = jnp.dot(cot, w_merge.T, preferred_element_type=jnp.float32) * merge_gain
    grad_z = (
        grad_n
        - jnp.mean(grad_n, axis=-1, keepdims=True)
        - unit * jnp.mean(grad_n * unit, axis=-1, keepdims=True)
    ) * inv
    grad_y = (
        grad_z.astype(jnp.bfloat16)
        .reshape(rows // 2, cols // 2, 2, 2, width)
        .transpose(0, 3, 1, 2, 4)
        .reshape(-1, width)
    )
    grad_d = jnp.dot(hidden.T, grad_y, preferred_element_type=jnp.float32)
    count = grad_m.size + grad_d.size
    sum_m, sum_d = lax.psum((grad_m, grad_d), ("row", "col"))
    total = jnp.sum(sum_m * sum_m) + jnp.sum(sum_d * sum_d)
    groups = lax.axis_size(("row", "col"))
    index = lax.axis_index(("row", "col"))
    share_m = lax.dynamic_slice_in_dim(
        sum_m, index * (sum_m.shape[0] // groups), sum_m.shape[0] // groups, 0
    )
    share_d = lax.dynamic_slice_in_dim(
        sum_d, index * (sum_d.shape[0] // groups), sum_d.shape[0] // groups, 0
    )
    factor = 1.0 / jnp.sqrt(total / count + 1e-06)
    return (merged, share_m * factor, share_d * factor)


def solution(mesh):
    placed = (
        P("row", "col", None),
        P(),
        P(),
        P(),
        P(),
        P(),
        P(),
        P(),
        P(),
        P(),
        P("row", "col", None),
    )
    return jax.shard_map(
        local,
        mesh=mesh,
        in_specs=placed,
        out_specs=(P("row", "col", None), P(("row", "col"), None), P(("row", "col"), None)),
        check_vma=False,
    )
```

profile of v0, /device:TPU:0, one launch (start us, length us, event | category | flops | bytes accessed | tf_op | source)
XLA Modules:
  0.0 520.5 jit_solution(10870981523958563618)
XLA Ops:
  13.7 3.9 copy.119
  20.2 5.8 %collective-permute-start = (bf16[3,1024,128]{2,1,0:T(8,128)(2,1)}, bf16[3,1024,128]{2,1,0:T(8,128)(2,1)}, u32[]{:S(2)}, u32[]{:S(2)}) collective-permute-start(bf16[3,1024,128]{2,1,0:T(8,128)(2,1)} %get-tuple-element.58), channel_id=1, source_target_pairs={{0,4},{4,8},{8,12},{12,16},{16,20},{20,24},{24,28},{1,5},{5,9},{9,... | collective-permute-start | bytes 2359304 | tf_op jit(solution)/shard_map/ppermute | solution.py:15
  39.6 19.4 %collective-permute-done = bf16[3,1024,128]{2,1,0:T(8,128)(2,1)} collective-permute-done((bf16[3,1024,128]{2,1,0:T(8,128)(2,1)}, bf16[3,1024,128]{2,1,0:T(8,128)(2,1)}, u32[]{:S(2)}, u32[]{:S(2)}) %collective-permute-start) | collective-permute-done | bytes 786464 | tf_op jit(solution)/shard_map/ppermute | solution.py:15
  60.6 4.3 fusion.140
  64.9 3.7 copy.120
  68.6 3.7 copy.121
  73.6 3.8 collective-permute-start.2
  78.2 3.9 copy.122
  82.1 3.1 copy.123
  85.2 8.4 %pad_maximum_fusion = bf16[14,1024,134]{2,1,0:T(8,128)(2,1)S(1)} fusion(bf16[14,1024,3]{2,1,0:T(8,128)(2,1)} %copy.123, bf16[3,1024,128]{2,1,0:T(8,128)(2,1)} %collective-permute-done.1, bf16[8,1024,128]{2,1,0:T(8,128)(2,1)} %bitcast.1631, bf16[3,1024,128]{2,1,0:T(8,128)(2,1)} %collective-permute-done, bf16[14,1024,3]{2,1,0:T(8,128)(2,1)} %copy.122), kind=kLoop, calls=%fused_computation.20 | loop fusion | flops 19210240 | bytes 7684096 | tf_op jit(solution)/shard_map/concatenate | solution.py:13
  93.6 7.9 %multiply_reduce_fusion.38 = (f32[8,16,128]{2,1,0:T(8,128)}, f32[8,16,128]{2,1,0:T(8,128)}, f32[8,16,128]{2,1,0:T(8,128)}, f32[8,16,128]{2,1,0:T(8,128)}, f32[8,...) fusion(bf16[14,2,16,32,134]{4,3,2,1,0:T(8,128)(2,1)S(1)} %bitca, ...), kind=kLoop, calls=%fused_computation.230 | loop fusion | flops 20234240 | bytes 16580608 | tf_op jit(solution)/shard_map/rhdc,rhdc->rhc/dot_general | solution.py:68
  101.5 12.3 %multiply_reduce_fusion.20 = (f32[8,16,128]{2,1,0:T(8,128)}, f32[8,16,128]{2,1,0:T(8,128)}, f32[8,16,128]{2,1,0:T(8,128)}, f32[8,16,128]{2,1,0:T(8,128)}, f32[8,...) fusion(bf16[14,2,16,32,134]{4,3,2,1,0:T(8,128)(2,1)S(1)} %bitca, ...), kind=kLoop, calls=%fused_computation.212 | loop fusion | flops 28016640 | bytes 22151168 | tf_op jit(solution)/shard_map/rhdc,rhdc->rhc/dot_general | solution.py:68
  113.8 11.8 %multiply_reduce_fusion.2 = (f32[8,16,128]{2,1,0:T(8,128)S(1)}, f32[8,16,128]{2,1,0:T(8,128)S(1)}, f32[8,16,128]{2,1,0:T(8,128)S(1)}, f32[8,16,128]{2,1,0:T(8,12...) fusion(bf16[14,2,16,32,134]{4,3,2,1,0:T(8,128)(2,1)S(1)} %bitca, ...), kind=kLoop, calls=%fused_computation.194 | loop fusion | flops 28016640 | bytes 22151168 | tf_op jit(solution)/shard_map/rhdc,rhdc->rhc/dot_general | solution.py:68
  146.0 43.3 %fusion.19 = bf16[8,128,16,32]{1,3,2,0:T(8,128)(2,1)} fusion(bf16[14,2,16,32,134]{4,3,2,1,0:T(8,128)(2,1)} %bitcast.1629, f32[8,128,16]{1,2,0:T(8,128)} %get-tuple-element.61, f32[8,128,16]{1,2,0:T(8,128)} %get-tuple-element.62, f32[8,128,16]{1,2,0:T(8,128)} %get-tuple-element.63, f32[8,128,16]{1,2,0:T(8,128)} %get-tuple-element.64, ...), kind=kLoop, calls=%fused_computation.40 | loop fusion | flops 77070336 | bytes 55640064 | tf_op jit(solution)/shard_map/convert_element_type | solution.py:89
  192.7 20.9 %fusion.2 = bf16[1024,2048]{1,0:T(8,128)(2,1)S(1)} fusion(bf16[512,2048]{1,0:T(8,128)(2,1)S(1)} %copy-done, bf16[1024,512]{1,0:T(8,128)(2,1)S(1)} %get-tuple-element.112, f32[512]{0:T(512)S(1)} %copy-done.35, f32[1024]{0:T(1024)S(1)} %add_sqrt_fusion, f32[1024]{0:T(1024)S(1)} %broadcast_multiply_fusion), kind=kOutput, calls=%fused_computation.3 | convolution fusion | flops 2286419968 | bytes 7350272 | tf_op jit(solution)/shard_map/dot_general | solution.py:95
  215.5 3.7 fusion.122
  223.5 4.1 multiply_reduce_fusion.52
  238.3 3.9 fusion.139
  252.1 6.8 %fusion.143 = f32[2048,512]{1,0:T(8,128)} fusion(bf16[1024,2048]{1,0:T(8,128)(2,1)} %copy-done.36, bf16[1024,512]{1,0:T(8,128)(2,1)} %reshape.2694), kind=kOutput, calls=%fused_computation.594 | convolution fusion | flops 2147483648 | bytes 9437184 | tf_op jit(solution)/shard_map/dot_general | solution.py:126
  259.0 4.5 fusion.142
  263.5 4.3 convolution_convert_fusion.2
  267.8 230.9 %all-reduce.3.cloned.1.call-done = (f32[2048,1024]{1,0:T(8,128)}, f32[2048,512]{1,0:T(8,128)}) async-done(((f32[2048,1024]{1,0:T(8,128)}, f32[2048,512]{1,0:T(8,128)}), (f32[2048,1024]{1,0:T(8,128)}, f32[2048,512]{1,0:T(8,128)})) %all-reduce.3.cloned.1.call-update) | async-done | bytes 12582928 | tf_op jit(solution)/shard_map/psum | solution.py:128
  498.7 3.9 multiply_reduce_fusion.1
  502.6 6.3 %multiply_reduce_fusion = f32[]{:T(128)} fusion(f32[2048,1024]{1,0:T(8,128)} %get-tuple-element.54), kind=kLoop, calls=%fused_computation.4 | loop fusion | flops 4194303 | bytes 8388612 | tf_op jit(solution)/shard_map/reduce_sum | solution.py:129
  (230 shorter events, 79.5 us)
Async XLA Ops:
  7.2 185.5 %copy-start = (bf16[512,2048]{1,0:T(8,128)(2,1)S(1)}, bf16[512,2048]{1,0:T(8,128)(2,1)}, u32[]{:S(2)}) copy-start(bf16[512,2048]{1,0:T(8,128)(2,1)} %param.17) | copy-start | bytes 6291460
  7.2 491.5 %all-reduce.3.cloned.1.call-start = ((), (), s32[]{:S(2)}) async-start(), calls=%async_computation | async-start | bytes 25165824 | tf_op jit(solution)/shard_map/psum | solution.py:128
  20.2 38.8 %collective-permute-start = (bf16[3,1024,128]{2,1,0:T(8,128)(2,1)}, bf16[3,1024,128]{2,1,0:T(8,128)(2,1)}, u32[]{:S(2)}, u32[]{:S(2)}) collective-permute-start(bf16[3,1024,128]{2,1,0:T(8,128)(2,1)} %get-tuple-element.58), channel_id=1, source_target_pairs={{0,4},{4,8},{8,12},{12,16},{16,20},{20,24},{24,28},{1,5},{5,9},{9,... | collective-permute-start | bytes 2359304 | tf_op jit(solution)/shard_map/ppermute | solution.py:15
  26.0 33.1 %collective-permute-start.1 = (bf16[3,1024,128]{2,1,0:T(8,128)(2,1)}, bf16[3,1024,128]{2,1,0:T(8,128)(2,1)}, u32[]{:S(2)}, u32[]{:S(2)}) collective-permute-start(bf16[3,1024,128]{2,1,0:T(8,128)(2,1)} %get-tuple-element.59), channel_id=1, source_target_pairs={{4,0},{8,4},{12,8},{16,12},{20,16},{24,20},{28,24},{5,1},{9,5},{13... | collective-permute-start | bytes 2359304 | tf_op jit(solution)/shard_map/ppermute | solution.py:17
  37.9 21.1 %copy-start.4 = (bf16[8,128,1024]{1,2,0:T(8,128)(2,1)S(1)}, bf16[8,128,1024]{1,2,0:T(8,128)(2,1)}, u32[]{:S(2)}) copy-start(bf16[8,128,1024]{1,2,0:T(8,128)(2,1)} %copy.119) | copy-start | bytes 6291460
  72.3 9.8 %collective-permute-start.3 = (bf16[14,1024,3]{1,0,2:T(8,128)(2,1)S(1)}, bf16[14,1024,3]{1,0,2:T(8,128)(2,1)S(1)}, u32[]{:S(2)}, u32[]{:S(2)}) collective-permute-start(bf16[14,1024,3]{1,0,2:T(8,128)(2,1)S(1)} %copy.121), channel_id=1, source_target_pairs={{1,0},{2,1},{3,2},{5,4},{6,5},{7,6},{9,8},{10,9},{11,10},{13,12},{... | collective-permute-start | bytes 258056 | tf_op jit(solution)/shard_map/ppermute | solution.py:17
  73.6 4.6 collective-permute-start.2
  93.6 20.2 %copy-start.2 = (bf16[14,1024,134]{2,1,0:T(8,128)(2,1)}, bf16[14,1024,134]{2,1,0:T(8,128)(2,1)S(1)}, u32[]{:S(2)}) copy-start(bf16[14,1024,134]{2,1,0:T(8,128)(2,1)S(1)} %pad_maximum_fusion) | copy-start | bytes 11526148
  125.6 13.9 %copy-start.24 = (f32[8,16,128]{2,1,0:T(8,128)S(1)}, f32[8,16,128]{2,1,0:T(8,128)}, u32[]{:S(2)}) copy-start(f32[8,16,128]{2,1,0:T(8,128)} %get-tuple-element.33) | copy-start | bytes 196612
  125.6 13.9 %copy-start.23 = (f32[8,16,128]{2,1,0:T(8,128)S(1)}, f32[8,16,128]{2,1,0:T(8,128)}, u32[]{:S(2)}) copy-start(f32[8,16,128]{2,1,0:T(8,128)} %get-tuple-element.32) | copy-start | bytes 196612
  125.6 14.0 %copy-start.22 = (f32[8,16,128]{2,1,0:T(8,128)S(1)}, f32[8,16,128]{2,1,0:T(8,128)}, u32[]{:S(2)}) copy-start(f32[8,16,128]{2,1,0:T(8,128)} %get-tuple-element.31) | copy-start | bytes 196612
  125.6 14.0 %copy-start.21 = (f32[8,16,128]{2,1,0:T(8,128)S(1)}, f32[8,16,128]{2,1,0:T(8,128)}, u32[]{:S(2)}) copy-start(f32[8,16,128]{2,1,0:T(8,128)} %get-tuple-element.30) | copy-start | bytes 196612
  125.6 14.0 %copy-start.20 = (f32[8,16,128]{2,1,0:T(8,128)S(1)}, f32[8,16,128]{2,1,0:T(8,128)}, u32[]{:S(2)}) copy-start(f32[8,16,128]{2,1,0:T(8,128)} %get-tuple-element.29) | copy-start | bytes 196612
  125.6 14.0 %copy-start.19 = (f32[8,16,128]{2,1,0:T(8,128)S(1)}, f32[8,16,128]{2,1,0:T(8,128)}, u32[]{:S(2)}) copy-start(f32[8,16,128]{2,1,0:T(8,128)} %get-tuple-element.28) | copy-start | bytes 196612
  125.6 14.0 %copy-start.18 = (f32[8,16,128]{2,1,0:T(8,128)S(1)}, f32[8,16,128]{2,1,0:T(8,128)}, u32[]{:S(2)}) copy-start(f32[8,16,128]{2,1,0:T(8,128)} %get-tuple-element.27) | copy-start | bytes 196612
  125.6 14.0 %copy-start.17 = (f32[8,16,128]{2,1,0:T(8,128)S(1)}, f32[8,16,128]{2,1,0:T(8,128)}, u32[]{:S(2)}) copy-start(f32[8,16,128]{2,1,0:T(8,128)} %get-tuple-element.26) | copy-start | bytes 196612
  125.6 14.0 %copy-start.16 = (f32[8,16,128]{2,1,0:T(8,128)S(1)}, f32[8,16,128]{2,1,0:T(8,128)}, u32[]{:S(2)}) copy-start(f32[8,16,128]{2,1,0:T(8,128)} %get-tuple-element.25) | copy-start | bytes 196612
  125.7 14.1 %copy-start.15 = (f32[8,16,128]{2,1,0:T(8,128)S(1)}, f32[8,16,128]{2,1,0:T(8,128)}, u32[]{:S(2)}) copy-start(f32[8,16,128]{2,1,0:T(8,128)} %get-tuple-element.24) | copy-start | bytes 196612
  125.7 14.1 %copy-start.14 = (f32[8,16,128]{2,1,0:T(8,128)S(1)}, f32[8,16,128]{2,1,0:T(8,128)}, u32[]{:S(2)}) copy-start(f32[8,16,128]{2,1,0:T(8,128)} %get-tuple-element.23) | copy-start | bytes 196612
  125.7 14.1 %copy-start.13 = (f32[8,16,128]{2,1,0:T(8,128)S(1)}, f32[8,16,128]{2,1,0:T(8,128)}, u32[]{:S(2)}) copy-start(f32[8,16,128]{2,1,0:T(8,128)} %get-tuple-element.22) | copy-start | bytes 196612
  125.7 14.1 %copy-start.12 = (f32[8,16,128]{2,1,0:T(8,128)S(1)}, f32[8,16,128]{2,1,0:T(8,128)}, u32[]{:S(2)}) copy-start(f32[8,16,128]{2,1,0:T(8,128)} %get-tuple-element.21) | copy-start | bytes 196612
  125.7 14.1 %copy-start.11 = (f32[8,16,128]{2,1,0:T(8,128)S(1)}, f32[8,16,128]{2,1,0:T(8,128)}, u32[]{:S(2)}) copy-start(f32[8,16,128]{2,1,0:T(8,128)} %get-tuple-element.20) | copy-start | bytes 196612
  125.7 14.1 %copy-start.10 = (f32[8,16,128]{2,1,0:T(8,128)S(1)}, f32[8,16,128]{2,1,0:T(8,128)}, u32[]{:S(2)}) copy-start(f32[8,16,128]{2,1,0:T(8,128)} %get-tuple-element.19) | copy-start | bytes 196612
  192.6 22.8 %copy-start.32 = (bf16[2048,512]{1,0:T(8,128)(2,1)S(1)}, bf16[2048,512]{1,0:T(8,128)(2,1)}, u32[]{:S(2)}) copy-start(bf16[2048,512]{1,0:T(8,128)(2,1)} %param.18) | copy-start | bytes 6291460
  (18 other events, 121.3 us)
Sparse Core Ops, SparseCore 0:
  263.6 235.0 all-reduce.2
where the time goes:
time: 527 us; the launch traced here: 521 us
  waiting for transfers between devices  250 us (47%)
  other arithmetic  125 us (24%)
  local copies, waits for them, and re-layouts  66.3 us (13%)
  matrix products  50.6 us (10%)
  between operations  16.6 us (3%)
  starting transfers between devices  12.2 us (2%)
    psum x1, waiting for transfers between devices, local(): sum_m, sum_d = lax.psum((grad_m, grad_d), ('row', 'col'))  231 us
    convert_element_type x1, other arithmetic, local(): attn = attn.astype(jnp.bfloat16).transpose(0, 3, 1, 2).reshape(-1, width)  43.3 us
    dot_general x3, other arithmetic, local(): jnp.einsum('rhdc,rhdc->rhc', query_t, key, preferred_element_type=jnp.flo...  31.9 us
    dot_general x1, matrix products, local(): jnp.dot(normed2, w_up, preferred_element_type=jnp.float32)  20.9 us
    ppermute x2, waiting for transfers between devices, with_halo(): lax.ppermute(tail, axis, [(i, (i + 1) % count) for i in range(ends)])  19.4 us
    unnamed x123, local copies, waits for them, and re-layouts  17.5 us
    slice x3, local copies, waits for them, and re-layouts, with_halo(): lax.slice_in_dim(cells, cells.shape[dim] - width, cells.shape[dim], axis=...  10.6 us
  transfers between devices with their start and end apart: 5, of which 2 were waited for; matrix products, arithmetic and copies ran while one was open for 4% of the time, Pallas kernels for 0%

commit v1 on v0

--- a/solution.py
+++ b/solution.py
@@ -125,7 +125,7 @@
     )
     grad_d = jnp.dot(hidden.T, grad_y, preferred_element_type=jnp.float32)
     count = grad_m.size + grad_d.size
-    sum_m, sum_d = lax.psum((grad_m, grad_d), ("row", "col"))
+    sum_m, sum_d = lax.psum(lax.psum((grad_m, grad_d), "col"), "row")
     total = jnp.sum(sum_m * sum_m) + jnp.sum(sum_d * sum_d)
     groups = lax.axis_size(("row", "col"))
     index = lax.axis_index(("row", "col"))

time: 527 us -> 917 us (1.74)
  waiting for transfers between devices: 250 us -> 639 us
    psum x1 -> x2, waiting for transfers between devices: 231 us -> 620 us  [local(): sum_m, sum_d = lax.psum(lax.psum((grad_m, grad_d), 'col'), 'row')]
  transfers between devices with their start and end apart: 5 -> 6, of which waited for: 2 -> 3; matrix products, arithmetic and copies ran while one was open for 4% -> 2% of each run, Pallas kernels for 0% -> 0%
where the time goes in v1:
time: 917 us; the launch traced here: 910 us
  waiting for transfers between devices  639 us (70%)
  other arithmetic  125 us (14%)
  local copies, waits for them, and re-layouts  66.1 us (7%)
  matrix products  50.6 us (6%)
  between operations  16.6 us (2%)
  starting transfers between devices  12.5 us (1%)
    psum x2, waiting for transfers between devices, local(): sum_m, sum_d = lax.psum(lax.psum((grad_m, grad_d), 'col'), 'row')  620 us
    convert_element_type x1, other arithmetic, local(): attn = attn.astype(jnp.bfloat16).transpose(0, 3, 1, 2).reshape(-1, width)  43.3 us
    dot_general x3, other arithmetic, local(): jnp.einsum('rhdc,rhdc->rhc', query_t, key, preferred_element_type=jnp.flo...  31.9 us
    dot_general x1, matrix products, local(): jnp.dot(normed2, w_up, preferred_element_type=jnp.float32)  20.9 us
    ppermute x2, waiting for transfers between devices, with_halo(): lax.ppermute(tail, axis, [(i, (i + 1) % count) for i in range(ends)])  19.4 us
  transfers between devices with their start and end apart: 6, of which 3 were waited for; matrix products, arithmetic and copies ran while one was open for 2% of the time, Pallas kernels for 0%

profile of v1, /device:TPU:0, one launch (start us, length us, event | category | flops | bytes accessed | tf_op | source)
XLA Modules:
  0.0 909.6 jit_solution(533474238255813847)
XLA Ops:
  13.7 3.9 copy.119
  20.2 5.8 collective-permute-start
  39.6 19.4 %collective-permute-done = bf16[3,1024,128]{2,1,0:T(8,128)(2,1)} collective-permute-done((bf16[3,1024,128]{2,1,0:T(8,128)(2,1)}, bf16[3,1024,128]{2,1,0:T(8,128)(2,1)}, u32[]{:S(2)}, u32[]{:S(2)}) %collective-permute-start) | collective-permute-done | bytes 786464 | tf_op jit(solution)/shard_map/ppermute | solution.py:15
  60.6 4.3 fusion.140
  64.9 3.7 copy.120
  68.6 3.7 copy.121
  73.6 3.8 collective-permute-start.2
  78.2 3.9 copy.122
  85.2 8.4 pad_maximum_fusion
  93.6 7.9 multiply_reduce_fusion.38
  101.5 12.3 %multiply_reduce_fusion.20 = (f32[8,16,128]{2,1,0:T(8,128)}, f32[8,16,128]{2,1,0:T(8,128)}, f32[8,16,128]{2,1,0:T(8,128)}, f32[8,16,128]{2,1,0:T(8,128)}, f32[8,...) fusion(bf16[14,2,16,32,134]{4,3,2,1,0:T(8,128)(2,1)S(1)} %bitca, ...), kind=kLoop, calls=%fused_computation.212 | loop fusion | flops 28016640 | bytes 22151168 | tf_op jit(solution)/shard_map/rhdc,rhdc->rhc/dot_general | solution.py:68
  113.8 11.8 %multiply_reduce_fusion.2 = (f32[8,16,128]{2,1,0:T(8,128)S(1)}, f32[8,16,128]{2,1,0:T(8,128)S(1)}, f32[8,16,128]{2,1,0:T(8,128)S(1)}, f32[8,16,128]{2,1,0:T(8,12...) fusion(bf16[14,2,16,32,134]{4,3,2,1,0:T(8,128)(2,1)S(1)} %bitca, ...), kind=kLoop, calls=%fused_computation.194 | loop fusion | flops 28016640 | bytes 22151168 | tf_op jit(solution)/shard_map/rhdc,rhdc->rhc/dot_general | solution.py:68
  146.0 43.3 %fusion.19 = bf16[8,128,16,32]{1,3,2,0:T(8,128)(2,1)} fusion(bf16[14,2,16,32,134]{4,3,2,1,0:T(8,128)(2,1)} %bitcast.1629, f32[8,128,16]{1,2,0:T(8,128)} %get-tuple-element.63, f32[8,128,16]{1,2,0:T(8,128)} %get-tuple-element.64, f32[8,128,16]{1,2,0:T(8,128)} %get-tuple-element.65, f32[8,128,16]{1,2,0:T(8,128)} %get-tuple-element.66, ...), kind=kLoop, calls=%fused_computation.40 | loop fusion | flops 77070336 | bytes 55640064 | tf_op jit(solution)/shard_map/convert_element_type | solution.py:89
  192.7 20.9 %fusion.2 = bf16[1024,2048]{1,0:T(8,128)(2,1)S(1)} fusion(bf16[512,2048]{1,0:T(8,128)(2,1)S(1)} %copy-done, bf16[1024,512]{1,0:T(8,128)(2,1)S(1)} %get-tuple-element.114, f32[512]{0:T(512)S(1)} %copy-done.35, f32[1024]{0:T(1024)S(1)} %add_sqrt_fusion, f32[1024]{0:T(1024)S(1)} %broadcast_multiply_fusion), kind=kOutput, calls=%fused_computation.3 | convolution fusion | flops 2286419968 | bytes 7350272 | tf_op jit(solution)/shard_map/dot_general | solution.py:95
  215.5 3.7 fusion.122
  223.5 4.1 multiply_reduce_fusion.52
  238.3 3.9 fusion.139
  251.9 6.9 fusion.143
  258.8 4.5 fusion.142
  263.6 225.0 %all-reduce.7.cloned.1.call-done = (f32[2048,1024]{1,0:T(8,128)}, f32[2048,512]{1,0:T(8,128)}) async-done(((f32[2048,1024]{1,0:T(8,128)}, f32[2048,512]{1,0:T(8,128)}), (f32[2048,1024]{1,0:T(8,128)}, f32[2048,512]{1,0:T(8,128)})) %all-reduce.7.cloned.1.call-update) | async-done | bytes 12582928 | tf_op jit(solution)/shard_map/psum | solution.py:128
  488.6 4.3 convolution_convert_fusion.2
  492.9 394.9 %all-reduce.5.cloned.1.call-done = (f32[2048,1024]{1,0:T(8,128)}, f32[2048,512]{1,0:T(8,128)}) async-done(((f32[2048,1024]{1,0:T(8,128)}, f32[2048,512]{1,0:T(8,128)}), (f32[2048,1024]{1,0:T(8,128)}, f32[2048,512]{1,0:T(8,128)})) %all-reduce.5.cloned.1.call-update) | async-done | bytes 12582928 | tf_op jit(solution)/shard_map/psum | solution.py:128
  887.8 3.9 multiply_reduce_fusion.1
  891.6 6.3 multiply_reduce_fusion
  (233 shorter events, 82.7 us)
Async XLA Ops:
  7.2 185.5 %copy-start = (bf16[512,2048]{1,0:T(8,128)(2,1)S(1)}, bf16[512,2048]{1,0:T(8,128)(2,1)}, u32[]{:S(2)}) copy-start(bf16[512,2048]{1,0:T(8,128)(2,1)} %param.17) | copy-start | bytes 6291460
  7.2 481.3 %all-reduce.7.cloned.1.call-start = ((), (), s32[]{:S(2)}) async-start(), calls=%async_computation.1 | async-start | bytes 25165824 | tf_op jit(solution)/shard_map/psum | solution.py:128
  20.2 38.8 %collective-permute-start = (bf16[3,1024,128]{2,1,0:T(8,128)(2,1)}, bf16[3,1024,128]{2,1,0:T(8,128)(2,1)}, u32[]{:S(2)}, u32[]{:S(2)}) collective-permute-start(bf16[3,1024,128]{2,1,0:T(8,128)(2,1)} %get-tuple-element.60), channel_id=1, source_target_pairs={{0,4},{4,8},{8,12},{12,16},{16,20},{20,24},{24,28},{1,5},{5,9},{9,... | collective-permute-start | bytes 2359304 | tf_op jit(solution)/shard_map/ppermute | solution.py:15
  26.0 33.1 %collective-permute-start.1 = (bf16[3,1024,128]{2,1,0:T(8,128)(2,1)}, bf16[3,1024,128]{2,1,0:T(8,128)(2,1)}, u32[]{:S(2)}, u32[]{:S(2)}) collective-permute-start(bf16[3,1024,128]{2,1,0:T(8,128)(2,1)} %get-tuple-element.61), channel_id=1, source_target_pairs={{4,0},{8,4},{12,8},{16,12},{20,16},{24,20},{28,24},{5,1},{9,5},{13... | collective-permute-start | bytes 2359304 | tf_op jit(solution)/shard_map/ppermute | solution.py:17
  37.9 21.1 %copy-start.4 = (bf16[8,128,1024]{1,2,0:T(8,128)(2,1)S(1)}, bf16[8,128,1024]{1,2,0:T(8,128)(2,1)}, u32[]{:S(2)}) copy-start(bf16[8,128,1024]{1,2,0:T(8,128)(2,1)} %copy.119) | copy-start | bytes 6291460
  72.3 9.8 %collective-permute-start.3 = (bf16[14,1024,3]{1,0,2:T(8,128)(2,1)S(1)}, bf16[14,1024,3]{1,0,2:T(8,128)(2,1)S(1)}, u32[]{:S(2)}, u32[]{:S(2)}) collective-permute-start(bf16[14,1024,3]{1,0,2:T(8,128)(2,1)S(1)} %copy.121), channel_id=1, source_target_pairs={{1,0},{2,1},{3,2},{5,4},{6,5},{7,6},{9,8},{10,9},{11,10},{13,12},{... | collective-permute-start | bytes 258056 | tf_op jit(solution)/shard_map/ppermute | solution.py:17
  73.6 4.6 collective-permute-start.2
  93.6 20.2 %copy-start.2 = (bf16[14,1024,134]{2,1,0:T(8,128)(2,1)}, bf16[14,1024,134]{2,1,0:T(8,128)(2,1)S(1)}, u32[]{:S(2)}) copy-start(bf16[14,1024,134]{2,1,0:T(8,128)(2,1)S(1)} %pad_maximum_fusion) | copy-start | bytes 11526148
  125.6 13.9 %copy-start.23 = (f32[8,16,128]{2,1,0:T(8,128)S(1)}, f32[8,16,128]{2,1,0:T(8,128)}, u32[]{:S(2)}) copy-start(f32[8,16,128]{2,1,0:T(8,128)} %get-tuple-element.32) | copy-start | bytes 196612
  125.6 14.0 %copy-start.22 = (f32[8,16,128]{2,1,0:T(8,128)S(1)}, f32[8,16,128]{2,1,0:T(8,128)}, u32[]{:S(2)}) copy-start(f32[8,16,128]{2,1,0:T(8,128)} %get-tuple-element.31) | copy-start | bytes 196612
  125.6 14.0 %copy-start.21 = (f32[8,16,128]{2,1,0:T(8,128)S(1)}, f32[8,16,128]{2,1,0:T(8,128)}, u32[]{:S(2)}) copy-start(f32[8,16,128]{2,1,0:T(8,128)} %get-tuple-element.30) | copy-start | bytes 196612
  125.6 14.0 %copy-start.20 = (f32[8,16,128]{2,1,0:T(8,128)S(1)}, f32[8,16,128]{2,1,0:T(8,128)}, u32[]{:S(2)}) copy-start(f32[8,16,128]{2,1,0:T(8,128)} %get-tuple-element.29) | copy-start | bytes 196612
  125.6 14.0 %copy-start.19 = (f32[8,16,128]{2,1,0:T(8,128)S(1)}, f32[8,16,128]{2,1,0:T(8,128)}, u32[]{:S(2)}) copy-start(f32[8,16,128]{2,1,0:T(8,128)} %get-tuple-element.28) | copy-start | bytes 196612
  125.6 14.0 %copy-start.18 = (f32[8,16,128]{2,1,0:T(8,128)S(1)}, f32[8,16,128]{2,1,0:T(8,128)}, u32[]{:S(2)}) copy-start(f32[8,16,128]{2,1,0:T(8,128)} %get-tuple-element.27) | copy-start | bytes 196612
  125.6 14.0 %copy-start.17 = (f32[8,16,128]{2,1,0:T(8,128)S(1)}, f32[8,16,128]{2,1,0:T(8,128)}, u32[]{:S(2)}) copy-start(f32[8,16,128]{2,1,0:T(8,128)} %get-tuple-element.26) | copy-start | bytes 196612
  125.6 14.0 %copy-start.16 = (f32[8,16,128]{2,1,0:T(8,128)S(1)}, f32[8,16,128]{2,1,0:T(8,128)}, u32[]{:S(2)}) copy-start(f32[8,16,128]{2,1,0:T(8,128)} %get-tuple-element.25) | copy-start | bytes 196612
  125.7 14.1 %copy-start.15 = (f32[8,16,128]{2,1,0:T(8,128)S(1)}, f32[8,16,128]{2,1,0:T(8,128)}, u32[]{:S(2)}) copy-start(f32[8,16,128]{2,1,0:T(8,128)} %get-tuple-element.24) | copy-start | bytes 196612
  125.7 14.1 %copy-start.14 = (f32[8,16,128]{2,1,0:T(8,128)S(1)}, f32[8,16,128]{2,1,0:T(8,128)}, u32[]{:S(2)}) copy-start(f32[8,16,128]{2,1,0:T(8,128)} %get-tuple-element.23) | copy-start | bytes 196612
  125.7 14.1 %copy-start.13 = (f32[8,16,128]{2,1,0:T(8,128)S(1)}, f32[8,16,128]{2,1,0:T(8,128)}, u32[]{:S(2)}) copy-start(f32[8,16,128]{2,1,0:T(8,128)} %get-tuple-element.22) | copy-start | bytes 196612
  125.7 14.1 %copy-start.12 = (f32[8,16,128]{2,1,0:T(8,128)S(1)}, f32[8,16,128]{2,1,0:T(8,128)}, u32[]{:S(2)}) copy-start(f32[8,16,128]{2,1,0:T(8,128)} %get-tuple-element.21) | copy-start | bytes 196612
  125.7 14.1 %copy-start.11 = (f32[8,16,128]{2,1,0:T(8,128)S(1)}, f32[8,16,128]{2,1,0:T(8,128)}, u32[]{:S(2)}) copy-start(f32[8,16,128]{2,1,0:T(8,128)} %get-tuple-element.20) | copy-start | bytes 196612
  125.7 14.1 %copy-start.10 = (f32[8,16,128]{2,1,0:T(8,128)S(1)}, f32[8,16,128]{2,1,0:T(8,128)}, u32[]{:S(2)}) copy-start(f32[8,16,128]{2,1,0:T(8,128)} %get-tuple-element.19) | copy-start | bytes 196612
  192.6 22.8 %copy-start.32 = (bf16[2048,512]{1,0:T(8,128)(2,1)S(1)}, bf16[2048,512]{1,0:T(8,128)(2,1)}, u32[]{:S(2)}) copy-start(bf16[2048,512]{1,0:T(8,128)(2,1)} %param.18) | copy-start | bytes 6291460
  263.3 624.4 %all-reduce.5.cloned.1.call-start = ((), (), s32[]{:S(2)}) async-start(), calls=%async_computation | async-start | bytes 25165824 | tf_op jit(solution)/shard_map/psum | solution.py:128
  (19 other events, 135.2 us)
Sparse Core Ops, SparseCore 0:
  263.5 225.0 all-reduce.6
  492.8 394.8 all-reduce.4
